TPU v7x, 256 devices: a whole 4x4x8 slice. The times are simulated.
256 devices in a mesh: dp: 8 (over z), expert: 8 (over x, core), tensor: 4 (over y).
Axes of the slice: x: 4, y: 4, z: 8, core: 2. Of those that a mesh axis runs over, the one named last changes fastest.
Arguments:
- skip_stream_entry: bfloat16 [4096, 4096], P(('dp', 'expert', 'tensor')), may hold values from -6 to 6
- question_vectors: bfloat16 [4096, 2048], P(('dp', 'expert'), 'tensor'), may hold values from -5 to 5
- fresh_lookup_vectors: bfloat16 [4096, 512], P(('dp', 'expert'), 'tensor'), may hold values from -5 to 5
- fresh_content_vectors: bfloat16 [4096, 512], P(('dp', 'expert'), 'tensor'), may hold values from -10 to 10
- stored_lookup_sheets: bfloat16 [2560, 4, 128, 128], P(('dp', 'expert'), 'tensor'), may hold values from -5 to 5
- stored_content_sheets: bfloat16 [2560, 4, 128, 128], P(('dp', 'expert'), 'tensor'), may hold values from -10 to 10
- sequence_sheet_map: int32 [1088, 8], P(('dp', 'expert')), may hold values from 0 to 39
- stored_position_counts: int32 [1088], P(('dp', 'expert')), may hold values from 2 to 1024
- attention_merge_matrix: bfloat16 [2048, 4096], P('tensor'), may hold values from -0.59765625 to 0.59765625
- premix_scale_factor: bfloat16 [4096], replicated, may hold values from 0.5 to 1.5
- chosen_specialists: int32 [4096, 2], P(('dp', 'expert', 'tensor')), may hold values from 0 to 7, all different within a row; in each aligned block of 16 rows (0 to 15, 16 to 31, ...) at most 6 rows name the same one
- selection_shares: float32 [4096, 2], P(('dp', 'expert', 'tensor')), may hold values from 0.2 to 1
- allowed_placements: int32 [8], replicated, may hold values from 2 to 3
- favored_specialist: int32 [1], replicated, may hold values from 0 to 7
- gating_matrices: bfloat16 [8, 7168, 4096], P('expert', ('dp', 'tensor')), may hold values from -0.09375 to 0.09375
- expand_matrices: bfloat16 [8, 7168, 4096], P('expert', ('dp', 'tensor')), may hold values from -0.09375 to 0.09375
- contract_matrices: bfloat16 [8, 7168, 4096], P('expert', ('dp', 'tensor')), may hold values from -0.0625 to 0.0625
Outputs:
- layer_out: bfloat16 [4096, 4096], P(('dp', 'expert', 'tensor'))
Inputs may be any that keep to these rules, and one draw needn't show every extreme that they name: `chosen_specialists`: in the 16 rows of one device no expert is named by more than 6 rows; a token names two different experts.
All inputs are finite; a program needn't handle non-finite values.
Results may differ from a plain program's by a relative error of at most 0.018.
Values may be sent and summed in bfloat16 or wider, within the bound.
A program may use at most 128 MiB of HBM per device.

v0:
```python
from functools import reduce
import math
import jax
import jax.numpy as jnp
from jax import lax
from jax.sharding import PartitionSpec as P

HD = 128
PLACEMENT_MOST = 6


def normalize(parts):
    highest = reduce(
        jnp.maximum,
        [
            jnp.max(jnp.where(visible, scores, -jnp.inf), axis=-1, keepdims=True)
            for scores, visible in parts
        ],
    )
    portions = [jnp.where(visible, jnp.exp(scores - highest), 0.0) for scores, visible in parts]
    denominator = reduce(
        jnp.add, [jnp.sum(portion, axis=-1, keepdims=True) for portion in portions]
    )
    return [(portion / denominator).astype(jnp.bfloat16) for portion in portions]


def attend(question_vectors, new_keys, new_values, key_pages, value_pages, table, spans):
    rows_all, head_count, head_width = question_vectors.shape
    kv_heads = new_keys.shape[1]
    group_size = head_count // kv_heads
    single_count = spans.shape[0] - 1
    page_count = table.shape[1]
    page_width = key_pages.shape[2]
    context = page_count * page_width
    inverse_root = 1.0 / math.sqrt(head_width)
    page_keys = key_pages[table]
    page_values = value_pages[table]
    grouped = question_vectors.reshape(rows_all, kv_heads, group_size, head_width)
    positions = jnp.arange(context, dtype=jnp.int32)
    single_q = grouped[:single_count]
    cache_dec = (
        jnp.einsum(
            "rkgh,rmkph->rkgmp",
            single_q,
            page_keys[:single_count],
            preferred_element_type=jnp.float32,
        ).reshape(single_count, kv_heads, group_size, context)
        * inverse_root
    )
    seen_dec = (positions[None, :] < spans[:single_count, None])[:, None, None, :]
    own_dec = (
        jnp.einsum(
            "rkgh,rkh->rkg", single_q, new_keys[:single_count], preferred_element_type=jnp.float32
        )[..., None]
        * inverse_root
    )
    weight_cache, weight_own = normalize(
        [(cache_dec, seen_dec), (own_dec, jnp.full(own_dec.shape, True))]
    )
    out_dec = jnp.einsum(
        "rkgmp,rmkph->rkgh",
        weight_cache.reshape(single_count, kv_heads, group_size, page_count, page_width),
        page_values[:single_count],
        preferred_element_type=jnp.float32,
    )
    out_dec = (
        out_dec
        + weight_own.astype(jnp.float32)
        * new_values[:single_count].astype(jnp.float32)[:, :, None, :]
    )
    prompt_q = grouped[single_count:]
    prompt_rows = rows_all - single_count
    cache_pro = (
        jnp.einsum(
            "rkgh,mkph->rkgmp",
            prompt_q,
            page_keys[single_count],
            preferred_element_type=jnp.float32,
        ).reshape(prompt_rows, kv_heads, group_size, context)
        * inverse_root
    )
    seen_pro = (positions < spans[single_count])[None, None, None, :]
    new_pro = (
        jnp.einsum(
            "rkgh,mkh->rkgm", prompt_q, new_keys[single_count:], preferred_element_type=jnp.float32
        )
        * inverse_root
    )
    prompt_index = jnp.arange(prompt_rows, dtype=jnp.int32)
    causal = (prompt_index[:, None] >= prompt_index[None, :])[:, None, None, :]
    weight_cpro, weight_npro = normalize([(cache_pro, seen_pro), (new_pro, causal)])
    out_pro = jnp.einsum(
        "rkgmp,mkph->rkgh",
        weight_cpro.reshape(prompt_rows, kv_heads, group_size, page_count, page_width),
        page_values[single_count],
        preferred_element_type=jnp.float32,
    )
    out_pro = out_pro + jnp.einsum(
        "rkgm,mkh->rkgh", weight_npro, new_values[single_count:], preferred_element_type=jnp.float32
    )
    joined = jnp.concatenate([out_dec, out_pro], axis=0).astype(jnp.bfloat16)
    return joined.reshape(rows_all, head_count * head_width)


def slot_table(member, ranking, keeping, slot_count):
    slot_hit = (
        ranking[:, :, None, None] == jnp.arange(slot_count, dtype=jnp.int32)[None, None, None, :]
    )
    return ((member[..., None] > 0) & keeping[:, :, None, None] & slot_hit).astype(jnp.bfloat16)


def expert_pass(send, gating_matrices, expand_matrices, contract_matrices):
    specialist_index, slot_count, model_width = send.shape
    holders = lax.axis_size("expert")
    local_count = gating_matrices.shape[0]
    arrived = lax.all_to_all(
        send.reshape(holders, local_count, slot_count, model_width),
        "expert",
        split_axis=0,
        concat_axis=0,
        tiled=True,
    )
    row_piece = lax.all_gather(arrived, ("dp", "tensor"), axis=0, tiled=True)
    gate_part = jnp.einsum(
        "qesd,efd->qesf", row_piece, gating_matrices, preferred_element_type=jnp.float32
    )
    up_part = jnp.einsum(
        "qesd,efd->qesf", row_piece, expand_matrices, preferred_element_type=jnp.float32
    )
    hidden = (jax.nn.silu(gate_part) * up_part).astype(jnp.bfloat16)
    summed = lax.psum_scatter(
        jnp.einsum(
            "qesf,efd->qesd", hidden, contract_matrices, preferred_element_type=jnp.float32
        ).astype(jnp.bfloat16),
        ("dp", "tensor"),
        scatter_dimension=0,
        tiled=True,
    )
    arrived_back = lax.all_to_all(summed, "expert", split_axis=0, concat_axis=0, tiled=True)
    return arrived_back.reshape(specialist_index, slot_count, model_width)


def local(
    skip_stream_entry,
    question_vectors,
    fresh_lookup_vectors,
    fresh_content_vectors,
    stored_lookup_sheets,
    stored_content_sheets,
    sequence_sheet_map,
    stored_position_counts,
    attention_merge_matrix,
    premix_scale_factor,
    chosen_specialists,
    selection_shares,
    allowed_placements,
    favored_specialist,
    gating_matrices,
    expand_matrices,
    contract_matrices,
):
    token_count = chosen_specialists.shape[0]
    specialist_index = allowed_placements.shape[0]
    picked = (
        chosen_specialists[:, :, None]
        == jnp.arange(specialist_index, dtype=jnp.int32)[None, None, :]
    ).astype(jnp.int32)
    flat_routes = picked.reshape(token_count * 2, specialist_index)
    busiest_specialist = favored_specialist[0]
    before = (jnp.cumsum(flat_routes, axis=0) - flat_routes).reshape(
        token_count, 2, specialist_index
    )
    ranking = jnp.sum(before * picked, axis=2)
    placement_ceiling = jnp.where(
        jnp.arange(specialist_index, dtype=jnp.int32) == busiest_specialist,
        PLACEMENT_MOST,
        allowed_placements,
    )
    keeping = ranking < jnp.sum(picked * placement_ceiling[None, None, :], axis=2)
    row_total = question_vectors.shape[0]
    heads_out = attend(
        question_vectors.reshape(row_total, -1, HD),
        fresh_lookup_vectors.reshape(row_total, -1, HD),
        fresh_content_vectors.reshape(row_total, -1, HD),
        stored_lookup_sheets,
        stored_content_sheets,
        sequence_sheet_map,
        stored_position_counts,
    )
    own_attn = lax.psum_scatter(
        jnp.dot(heads_out, attention_merge_matrix, preferred_element_type=jnp.float32).astype(
            jnp.bfloat16
        ),
        "tensor",
        scatter_dimension=0,
        tiled=True,
    ).astype(jnp.float32)
    stream = (skip_stream_entry.astype(jnp.float32) + own_attn).astype(jnp.bfloat16)
    wide = stream.astype(jnp.float32)
    squares = jnp.mean(wide * wide, axis=1, keepdims=True)
    normed = (wide * lax.rsqrt(squares + 1e-05) * premix_scale_factor.astype(jnp.float32)).astype(
        jnp.bfloat16
    )
    main_slots = PLACEMENT_MOST
    table_main = slot_table(picked, ranking, keeping, main_slots)
    send = jnp.einsum(
        "nkes,nd->esd", table_main, normed, preferred_element_type=jnp.float32
    ).astype(jnp.bfloat16)
    expert_out = expert_pass(send, gating_matrices, expand_matrices, contract_matrices)
    chosen = jnp.einsum("nkes,esd->nkd", table_main, expert_out, preferred_element_type=jnp.float32)
    mixed = jnp.sum(selection_shares[:, :, None] * chosen, axis=1)
    return (wide + mixed).astype(jnp.bfloat16)


def solution(mesh):
    placed = (
        P(("dp", "expert", "tensor"), None),
        P(("dp", "expert"), "tensor"),
        P(("dp", "expert"), "tensor"),
        P(("dp", "expert"), "tensor"),
        P(("dp", "expert"), "tensor", None, None),
        P(("dp", "expert"), "tensor", None, None),
        P(("dp", "expert"), None),
        P(("dp", "expert")),
        P("tensor", None),
        P(),
        P(("dp", "expert", "tensor"), None),
        P(("dp", "expert", "tensor"), None),
        P(),
        P(),
        P("expert", ("dp", "tensor"), None),
        P("expert", ("dp", "tensor"), None),
        P("expert", ("dp", "tensor"), None),
    )
    return jax.shard_map(
        local,
        mesh=mesh,
        in_specs=placed,
        out_specs=P(("dp", "expert", "tensor"), None),
        check_vma=False,
    )
```

profile of v0, /device:TPU:1, one launch (start us, length us, event | category | flops | bytes accessed | tf_op | source)
XLA Modules:
  0.0 500.2 jit_solution(16697747358621664481)
XLA Ops:
  7.4 1.2 slice.49
  8.7 1.2 broadcast_compare_fusion.1
  10.5 1.3 slice_bitcast_fusion.5
  12.0 1.3 slice_convert_fusion
  13.3 1.6 select_reduce_fusion.2
  14.8 8.8 %gather_fusion.1 = bf16[136,128,128]{2,1,0:T(8,128)(2,1)} fusion(bf16[40,128,128]{2,1,0:T(8,128)(2,1)} %bitcast.233, s32[1024]{0:T(1024)S(1)} %pad_clamp_fusion), kind=kCustom, calls=%fused_computation.1 | custom fusion | bytes 8913440 | tf_op jit(solution)/shard_map/gather | solution.py:37
  23.7 1.3 copy-done.2
  25.0 7.5 %gather_fusion = bf16[136,128,128]{2,1,0:T(8,128)(2,1)} fusion(bf16[40,128,128]{2,1,0:T(8,128)(2,1)S(1)} %bitcast.234, s32[1024]{0:T(1024)S(1)} %pad_clamp_fusion), kind=kCustom, calls=%fused_computation | custom fusion | bytes 8913440 | tf_op jit(solution)/shard_map/gather | solution.py:36
  33.4 1.7 select_reduce_fusion
  36.4 1.3 select_reduce_fusion.1
  38.0 1.4 slice-done.2
  40.1 1.6 convolution_convert_fusion
  43.4 24.8 %reduce-scatter.5.cloned.1.call-done = bf16[16,4096]{1,0:T(8,128)(2,1)} async-done(((bf16[64,4096]{1,0:T(8,128)(2,1)}), bf16[16,4096]{1,0:T(8,128)(2,1)}) %reduce-scatter.5.cloned.1.call-update) | async-done | bytes 131088 | tf_op jit(solution)/shard_map/reduce_scatter | solution.py:190
  68.1 1.1 fusion.53
  69.2 1.2 fusion.5
  70.6 15.7 %all_to_all.10 = bf16[8,1,6,4096]{3,2,1,0:T(8,128)(2,1)S(1)} all-to-all(bf16[8,1,6,4096]{3,2,1,0:T(8,128)(2,1)S(1)} %copy.41), channel_id=1, replica_groups=mesh['dp'=8,'expert'=8,'tensor'=4] {'expert'}, dimensions={0} | all-to-all | bytes 786432 | tf_op jit(solution)/shard_map/all_to_all | solution.py:116
  86.4 1.0 copy.42
  87.6 117.5 %all-gather.2.cloned.1.call-done = bf16[256,1,6,4096]{3,0,2,1:T(8,128)(2,1)} async-done(((bf16[8,1,6,4096]{3,0,2,1:T(8,128)(2,1)}), bf16[256,1,6,4096]{3,0,2,1:T(8,128)(2,1)}) %all-gather.2.cloned.1.call-update) | async-done | bytes 12582928 | tf_op jit(solution)/shard_map/all_gather | solution.py:123
  205.1 7.5 %fusion.9 = f32[256,1,6,224]{0,3,2,1:T(8,128)S(1)} fusion(bf16[1,224,4096]{2,1,0:T(8,128)(2,1)} %param.31, bf16[256,1,6,4096]{3,0,2,1:T(8,128)(2,1)} %all-gather.2.cloned.1.call-done), kind=kOutput, calls=%fused_computation.15 | convolution fusion | flops 2818572288 | bytes 15794176 | tf_op jit(solution)/shard_map/qesd,efd->qesf/dot_general | solution.py:124
  212.6 19.3 %fusion.97 = bf16[32,8,6,4096]{3,1,0,2:T(8,128)(2,1)} fusion(bf16[1,224,4096]{2,1,0:T(8,128)(2,1)S(1)} %copy-done, bf16[1,224,4096]{2,1,0:T(8,128)(2,1)} %param.32, bf16[256,1,6,4096]{3,0,2,1:T(8,128)(2,1)} %all-gather.2.cloned.1.call-done, f32[256,1,6,224]{0,3,2,1:T(8,128)S(1)} %fusion.9), kind=kOutput, calls=%fused_computation.124 | convolution fusion | flops 5645500416 | bytes 30212096 | tf_op jit(solution)/shard_map/qesf,efd->qesd/dot_general | solution.py:132
  231.9 10.6 %copy.58 = bf16[32,8,6,4096]{3,1,2,0:T(8,128)(2,1)} copy(bf16[32,8,6,4096]{3,1,0,2:T(8,128)(2,1)} %fusion.97) | data formatting | bytes 25165824
  242.6 230.3 %reduce-scatter.7.cloned.1.call-done = bf16[8,24576]{1,0:T(8,128)(2,1)} async-done(((bf16[256,24576]{1,0:T(8,128)(2,1)}), bf16[8,24576]{1,0:T(8,128)(2,1)}) %reduce-scatter.7.cloned.1.call-update) | async-done | bytes 393232
  472.9 1.2 copy.43
  474.1 18.4 %all_to_all.11 = bf16[8,1,6,4096]{3,2,1,0:T(8,128)(2,1)S(1)} all-to-all(bf16[8,1,6,4096]{3,2,1,0:T(8,128)(2,1)S(1)} %copy.43), channel_id=1, replica_groups=mesh['dp'=8,'expert'=8,'tensor'=4] {'expert'}, dimensions={0} | all-to-all | bytes 786432 | tf_op jit(solution)/shard_map/all_to_all | solution.py:139
  (89 shorter events, 7.2 us)
Async XLA Ops:
  6.5 206.1 %copy-start = (bf16[1,224,4096]{2,1,0:T(8,128)(2,1)S(1)}, bf16[1,224,4096]{2,1,0:T(8,128)(2,1)}, u32[]{:S(2)}) copy-start(bf16[1,224,4096]{2,1,0:T(8,128)(2,1)} %param.33) | copy-start | bytes 5505028
  6.5 61.6 %reduce-scatter.5.cloned.1.call-start = ((), (), s32[]{:S(2)}) async-start(), calls=%async_computation.4 | async-start | bytes 655360 | tf_op jit(solution)/shard_map/reduce_scatter | solution.py:190
  23.7 1.3 copy-start.2
  25.0 10.7 %slice-start = ((s8[4456448]{0:T(1024)(128)(4,1)}), s8[262144]{0:T(1024)(128)(4,1)S(1)}, s32[]{:S(2)}) async-start(s8[4456448]{0:T(1024)(128)(4,1)} %bitcast.229), calls=%async_computation.7 | async-start | bytes 524288
  32.5 0.8 copy-start.9
  32.5 0.8 copy-start.13
  32.6 2.6 copy-start.11
  32.6 2.9 copy-start.14
  32.6 3.1 slice-start.1
  33.4 2.7 copy-start.15
  33.4 2.8 copy-start.10
  33.4 3.0 slice-start.3
  35.7 3.6 slice-start.2
  35.7 3.6 copy-start.8
  36.4 3.8 copy-start.3
  39.3 2.5 copy-start.6
  39.3 3.8 copy-start.7
  39.3 3.8 copy-start.16
  39.4 28.8 %copy-start.4 = (bf16[16,4096]{1,0:T(8,128)(2,1)S(1)}, bf16[16,4096]{1,0:T(8,128)(2,1)}, u32[]{:S(2)}) copy-start(bf16[16,4096]{1,0:T(8,128)(2,1)} %param.17) | copy-start | bytes 393220
  41.8 163.3 %all-gather.2.cloned.1.call-start = ((), (), s32[]{:S(2)}) async-start(), calls=%async_computation.5 | async-start | bytes 12976128 | tf_op jit(solution)/shard_map/all_gather | solution.py:123
  87.4 385.5 %reduce-scatter.7.cloned.1.call-start = ((), (), s32[]{:S(2)}) async-start(), calls=%async_computation.6 | async-start | bytes 12976128
  242.5 250.0 %copy-start.12 = (f32[16,2]{0,1:T(2,128)S(1)}, f32[16,2]{0,1:T(2,128)}, u32[]{:S(2)}) copy-start(f32[16,2]{0,1:T(2,128)} %param.28) | copy-start | bytes 388
  242.5 250.4 %copy-start.5 = (bf16[16,4096]{1,0:T(8,128)(2,1)S(1)}, bf16[16,4096]{1,0:T(8,128)(2,1)}, u32[]{:S(2)}) copy-start(bf16[16,4096]{1,0:T(8,128)(2,1)} %reduce-scatter.5.cloned.1.call-done) | copy-start | bytes 393220
  242.6 251.1 %copy-start.1 = (bf16[1,224,4096]{2,1,0:T(8,128)(2,1)S(1)}, bf16[1,224,4096]{2,1,0:T(8,128)(2,1)}, u32[]{:S(2)}) copy-start(bf16[1,224,4096]{2,1,0:T(8,128)(2,1)} %param.33) | copy-start | bytes 5505028
Sparse Core Ops, SparseCore 0:
  41.9 26.1 reduce-scatter.4
  87.5 117.5 all-gather.1
  242.7 230.1 reduce-scatter.6
where the time goes:
time: 501 us; the launch traced here: 500 us
  waiting for transfers between devices  373 us (74%)
  local copies, waits for them, and re-layouts  36.9 us (7%)
  matrix products  35.9 us (7%)
  blocking collectives  34.2 us (7%)
  between operations  14.1 us (3%)
  other arithmetic  6.11 us (1%)
    unnamed x4, waiting for transfers between devices  230 us
    all_gather x1, waiting for transfers between devices, expert_pass(): row_piece = lax.all_gather(arrived, ('dp', 'tensor'), axis=0, tiled=True)  118 us
    reduce_scatter x1, waiting for transfers between devices, local(): lax.psum_scatter(jnp.dot(heads_out, attention_merge_matrix, preferred_ele...  24.8 us
    dot_general x1, matrix products, expert_pass(): jnp.einsum('qesf,efd->qesd', hidden, contract_matrices, preferred_element...  19.3 us
    all_to_all x1, blocking collectives, expert_pass(): lax.all_to_all(summed, 'expert', split_axis=0, concat_axis=0, tiled=True)  18.4 us
    all_to_all x1, blocking collectives, expert_pass(): lax.all_to_all(send.reshape(holders, local_count, slot_count, model_width...  15.7 us
    unnamed x42, local copies, waits for them, and re-layouts  12.9 us
  transfers between devices with their start and end apart: 3, of which 3 were waited for; matrix products, arithmetic and copies ran while one was open for 0% of the time, Pallas kernels for 0%

commit v1 on v0

--- a/solution.py
+++ b/solution.py
@@ -120,7 +120,9 @@
         concat_axis=0,
         tiled=True,
     )
-    row_piece = lax.all_gather(arrived, ("dp", "tensor"), axis=0, tiled=True)
+    earlier = jnp.stack([arrived for _ in range(lax.axis_size(("dp", "tensor")))], 0)
+    row_out = lax.all_to_all(earlier, ("dp", "tensor"), 0, 0)
+    row_piece = jnp.concatenate(row_out, 0)
     gate_part = jnp.einsum(
         "qesd,efd->qesf", row_piece, gating_matrices, preferred_element_type=jnp.float32
     )

time: 501 us -> 671 us (1.34)
  blocking collectives: 34.2 us -> 315 us
  waiting for transfers between devices: 373 us -> 256 us
  local copies, waits for them, and re-layouts: 36.9 us -> 46.8 us
    all_to_all x0 -> x1, blocking collectives: none -> 281 us  [expert_pass(): row_out = lax.all_to_all(earlier, ('dp', 'tensor'), 0, 0)]
    all_gather x1 -> x0, waiting for transfers between devices: 118 us -> none  [expert_pass(): row_piece = lax.all_gather(arrived, ('dp', 'tensor'), axis=0, tiled=True)]
    unnamed x42 -> x46, local copies, waits for them, and re-layouts: 12.9 us -> 17.4 us
    unnamed x4 -> x3, waiting for transfers between devices: 230 us -> 231 us
  transfers between devices with their start and end apart: 3 -> 2, of which waited for: 3 -> 2; matrix products, arithmetic and copies ran while one was open for 0% -> 0% of each run, Pallas kernels for 0% -> 0%
where the time goes in v1:
time: 671 us; the launch traced here: 670 us
  blocking collectives  315 us (47%)
  waiting for transfers between devices  256 us (38%)
  local copies, waits for them, and re-layouts  46.8 us (7%)
  matrix products  32.4 us (5%)
  between operations  14.4 us (2%)
    all_to_all x1, blocking collectives, expert_pass(): row_out = lax.all_to_all(earlier, ('dp', 'tensor'), 0, 0)  281 us
    unnamed x3, waiting for transfers between devices  231 us
    reduce_scatter x1, waiting for transfers between devices, local(): lax.psum_scatter(jnp.dot(heads_out, attention_merge_matrix, preferred_ele...  24.8 us
    dot_general x1, matrix products, expert_pass(): jnp.einsum('qesf,efd->qesd', hidden, contract_matrices, preferred_element...  19.4 us
    all_to_all x1, blocking collectives, expert_pass(): lax.all_to_all(summed, 'expert', split_axis=0, concat_axis=0, tiled=True)  18.3 us
    unnamed x46, local copies, waits for them, and re-layouts  17.4 us
    all_to_all x1, blocking collectives, expert_pass(): lax.all_to_all(send.reshape(holders, local_count, slot_count, model_width...  15.7 us
  transfers between devices with their start and end apart: 2, of which 2 were waited for; matrix products, arithmetic and copies ran while one was open for 0% of the time, Pallas kernels for 0%

profile of v1, /device:TPU:1, one launch (start us, length us, event | category | flops | bytes accessed | tf_op | source)
XLA Modules:
  0.0 670.5 jit_solution(5575072553941243543)
XLA Ops:
  7.4 1.2 slice.49
  8.7 1.2 broadcast_compare_fusion.1
  10.5 1.3 slice_bitcast_fusion.5
  12.0 1.3 slice_convert_fusion
  13.3 1.6 select_reduce_fusion.2
  14.8 8.8 %gather_fusion.1 = bf16[136,128,128]{2,1,0:T(8,128)(2,1)} fusion(bf16[40,128,128]{2,1,0:T(8,128)(2,1)} %bitcast.234, s32[1024]{0:T(1024)S(1)} %pad_clamp_fusion), kind=kCustom, calls=%fused_computation.1 | custom fusion | bytes 8913440 | tf_op jit(solution)/shard_map/gather | solution.py:37
  23.7 1.3 copy-done.2
  25.0 7.5 %gather_fusion = bf16[136,128,128]{2,1,0:T(8,128)(2,1)} fusion(bf16[40,128,128]{2,1,0:T(8,128)(2,1)S(1)} %bitcast.235, s32[1024]{0:T(1024)S(1)} %pad_clamp_fusion), kind=kCustom, calls=%fused_computation | custom fusion | bytes 8913440 | tf_op jit(solution)/shard_map/gather | solution.py:36
  33.4 1.7 select_reduce_fusion
  36.4 1.3 select_reduce_fusion.1
  38.0 1.4 slice-done.2
  40.1 1.6 convolution_convert_fusion
  43.4 24.8 %reduce-scatter.5.cloned.1.call-done = bf16[16,4096]{1,0:T(8,128)(2,1)} async-done(((bf16[64,4096]{1,0:T(8,128)(2,1)}), bf16[16,4096]{1,0:T(8,128)(2,1)}) %reduce-scatter.5.cloned.1.call-update) | async-done | bytes 131088 | tf_op jit(solution)/shard_map/reduce_scatter | solution.py:192
  69.2 1.2 fusion.7
  70.6 15.7 %all_to_all.18 = bf16[8,1,6,4096]{3,2,1,0:T(8,128)(2,1)S(1)} all-to-all(bf16[8,1,6,4096]{3,2,1,0:T(8,128)(2,1)S(1)} %copy.41), channel_id=1, replica_groups=mesh['dp'=8,'expert'=8,'tensor'=4] {'expert'}, dimensions={0} | all-to-all | bytes 786432 | tf_op jit(solution)/shard_map/all_to_all | solution.py:116
  86.6 6.2 stack.2
  92.8 281.1 %all_to_all.19 = bf16[32,8,1,6,4096]{4,1,3,2,0:T(8,128)(2,1)S(1)} all-to-all(bf16[32,8,1,6,4096]{4,1,3,2,0:T(8,128)(2,1)} %stack.2), channel_id=1, replica_groups=mesh['dp'=8,'expert'=8,'tensor'=4] {'dp','tensor'}, dimensions={0} | all-to-all | bytes 25165824 | tf_op jit(solution)/shard_map/all_to_all | solution.py:124
  373.8 4.5 copy-done.3
  378.3 3.8 fusion.11
  382.1 19.4 %fusion.98 = bf16[32,8,6,4096]{3,1,0,2:T(8,128)(2,1)} fusion(bf16[1,224,4096]{2,1,0:T(8,128)(2,1)S(1)} %copy-done, bf16[1,224,4096]{2,1,0:T(8,128)(2,1)} %param.32, bf16[32,8,1,6,4096]{4,1,3,2,0:T(8,128)(2,1)} %copy-done.3, f32[256,1,6,224]{0,3,2,1:T(8,128)S(1)} %fusion.11), kind=kOutput, calls=%fused_computation.125 | convolution fusion | flops 5645500416 | bytes 30212096 | tf_op jit(solution)/shard_map/qesf,efd->qesd/dot_general | solution.py:134
  401.6 10.6 %copy.59 = bf16[32,8,6,4096]{3,1,2,0:T(8,128)(2,1)} copy(bf16[32,8,6,4096]{3,1,0,2:T(8,128)(2,1)} %fusion.98) | data formatting | bytes 25165824
  412.2 230.8 %reduce-scatter.7.cloned.1.call-done = bf16[8,24576]{1,0:T(8,128)(2,1)} async-done(((bf16[256,24576]{1,0:T(8,128)(2,1)}), bf16[8,24576]{1,0:T(8,128)(2,1)}) %reduce-scatter.7.cloned.1.call-update) | async-done | bytes 393232
  643.0 1.2 copy.44
  644.3 18.3 %all_to_all.20 = bf16[8,1,6,4096]{3,2,1,0:T(8,128)(2,1)S(1)} all-to-all(bf16[8,1,6,4096]{3,2,1,0:T(8,128)(2,1)S(1)} %copy.44), channel_id=1, replica_groups=mesh['dp'=8,'expert'=8,'tensor'=4] {'expert'}, dimensions={0} | all-to-all | bytes 786432 | tf_op jit(solution)/shard_map/all_to_all | solution.py:141
  (92 shorter events, 8.3 us)
Async XLA Ops:
  6.5 375.6 %copy-start = (bf16[1,224,4096]{2,1,0:T(8,128)(2,1)S(1)}, bf16[1,224,4096]{2,1,0:T(8,128)(2,1)}, u32[]{:S(2)}) copy-start(bf16[1,224,4096]{2,1,0:T(8,128)(2,1)} %param.33) | copy-start | bytes 5505028
  6.5 61.6 %reduce-scatter.5.cloned.1.call-start = ((), (), s32[]{:S(2)}) async-start(), calls=%async_computation.5 | async-start | bytes 655360 | tf_op jit(solution)/shard_map/reduce_scatter | solution.py:192
  23.7 1.3 copy-start.2
  25.0 10.7 %slice-start = ((s8[4456448]{0:T(1024)(128)(4,1)}), s8[262144]{0:T(1024)(128)(4,1)S(1)}, s32[]{:S(2)}) async-start(s8[4456448]{0:T(1024)(128)(4,1)} %bitcast.230), calls=%async_computation.7 | async-start | bytes 524288
  32.5 0.8 copy-start.10
  32.6 2.6 copy-start.12
  32.6 2.9 copy-start.15
  32.6 3.1 slice-start.1
  33.4 2.7 copy-start.16
  33.4 2.8 copy-start.11
  33.4 3.0 slice-start.3
  35.7 3.6 slice-start.2
  35.7 3.6 copy-start.9
  36.4 3.8 copy-start.4
  39.3 2.5 copy-start.7
  39.3 3.8 copy-start.8
  39.3 3.8 copy-start.18
  39.4 28.8 %copy-start.5 = (bf16[16,4096]{1,0:T(8,128)(2,1)S(1)}, bf16[16,4096]{1,0:T(8,128)(2,1)}, u32[]{:S(2)}) copy-start(bf16[16,4096]{1,0:T(8,128)(2,1)} %param.17) | copy-start | bytes 393220
  41.8 601.2 %reduce-scatter.7.cloned.1.call-start = ((), (), s32[]{:S(2)}) async-start(), calls=%async_computation.6 | async-start | bytes 12976128
  92.8 285.5 %copy-start.17 = (bf16[1,224,4096]{2,1,0:T(8,128)(2,1)S(1)}, bf16[1,224,4096]{2,1,0:T(8,128)(2,1)}, u32[]{:S(2)}) copy-start(bf16[1,224,4096]{2,1,0:T(8,128)(2,1)} %param.31) | copy-start | bytes 5505028
  373.8 4.5 copy-start.3
  412.2 250.4 %copy-start.13 = (f32[16,2]{0,1:T(2,128)S(1)}, f32[16,2]{0,1:T(2,128)}, u32[]{:S(2)}) copy-start(f32[16,2]{0,1:T(2,128)} %param.28) | copy-start | bytes 388
  412.2 250.8 %copy-start.6 = (bf16[16,4096]{1,0:T(8,128)(2,1)S(1)}, bf16[16,4096]{1,0:T(8,128)(2,1)}, u32[]{:S(2)}) copy-start(bf16[16,4096]{1,0:T(8,128)(2,1)} %reduce-scatter.5.cloned.1.call-done) | copy-start | bytes 393220
  412.2 251.4 %copy-start.1 = (bf16[1,224,4096]{2,1,0:T(8,128)(2,1)S(1)}, bf16[1,224,4096]{2,1,0:T(8,128)(2,1)}, u32[]{:S(2)}) copy-start(bf16[1,224,4096]{2,1,0:T(8,128)(2,1)} %param.33) | copy-start | bytes 5505028
  (1 other events, 0.8 us)
Sparse Core Ops, SparseCore 0:
  41.9 26.1 reduce-scatter.4
  412.3 230.6 reduce-scatter.6
